TPU v7x, 32 devices: a whole 2x2x4 slice. The times are simulated.
32 devices in a mesh: expert: 4 (over y, core), dp: 8 (over z, x).
Axes of the slice: x: 2, y: 2, z: 4, core: 2. Of those that a mesh axis runs over, the one named last changes fastest.
Arguments:
- out_grad: bfloat16 [4096, 2048], P(('dp', 'expert')), parts along dimension 0, may hold values from -6 to 6
- route_ids: int32 [4096, 8], P(('dp', 'expert')), parts along dimension 0, may hold values from 0 to 31, as said below
- combine: float32 [4096, 8], P(('dp', 'expert')), parts along dimension 0, may hold values from 0.25 to 1
- row_lists: int32 [16, 4, 192], P('dp', None, 'expert'), parts along dimension 0, may hold values from -1 to 127, as said below
- saved_inputs: bfloat16 [16, 4, 192, 2048], P('dp', 'expert'), parts along dimension 0, may hold values from -6 to 6
- gate_weight: bfloat16 [4, 2048, 384], P('expert'), may hold values from -0.125 to 0.125
- up_weight: bfloat16 [4, 2048, 384], P('expert'), may hold values from -0.125 to 0.125
- down_weight: bfloat16 [4, 384, 2048], P('expert'), may hold values from -0.3125 to 0.3125
Outputs:
- input_grad: bfloat16 [4096, 2048], P(('dp', 'expert')), parts along dimension 0
There are 8 independent parts, one for each index of `dp`. A program takes and returns all parts, laid end to end along the dimension named above; an argument that names none is the same for every part. Nothing has to cross between parts.
Inputs may be any that keep to these rules, and one draw needn't show every extreme that they name: `route_ids`: each row names 8 different experts; expert e below 4 is held at index e of the expert axis, the others are outside this window. `row_lists`: entry [m, e, s * 48 + p] is -1 (empty) or the index, among the 128 tokens at index s of the expert axis, of a token of micro-batch m (index divided by 64 equals m) whose route_ids name e. Within each aligned block of 48 entries the indices rise and empty entries come last; a token stands at most once in the lists of one expert. Tokens naming e beyond 48 from one index in one micro-batch are left out. In every micro-batch some expert's block has all 192 entries filled.
All inputs are finite; a program needn't handle non-finite values.
Results may differ from a plain program's by a relative error of at most 0.0062.
Values may be sent and summed in bfloat16 or wider, within the bound.
A program may use at most 64 MiB of HBM per device.

v0:
```python
import jax
import jax.numpy as jnp
from jax import lax
from jax.sharding import PartitionSpec as P


def expert_backward(saved_rows, weighted, gate_weight, up_weight, down_weight):
    contract = (((1,), (1,)), ((), ()))
    gate_value = jnp.dot(saved_rows, gate_weight, preferred_element_type=jnp.float32)
    up_value = jnp.dot(saved_rows, up_weight, preferred_element_type=jnp.float32)
    grad_hidden = lax.dot_general(
        weighted, down_weight, contract, preferred_element_type=jnp.float32
    )
    sigmoid_gate = jax.nn.sigmoid(gate_value)
    silu_gate = gate_value * sigmoid_gate
    grad_gate = (
        grad_hidden * up_value * sigmoid_gate * (1.0 + gate_value * (1.0 - sigmoid_gate))
    ).astype(jnp.bfloat16)
    grad_up = (grad_hidden * silu_gate).astype(jnp.bfloat16)
    slot_grad = lax.dot_general(
        grad_gate, gate_weight, contract, preferred_element_type=jnp.float32
    )
    slot_grad = slot_grad + lax.dot_general(
        grad_up, up_weight, contract, preferred_element_type=jnp.float32
    )
    return slot_grad.astype(jnp.bfloat16)


def token_weights(route_ids, combine, experts):
    window_ids = jnp.arange(experts, dtype=jnp.int32)
    named = route_ids[:, :, None] == window_ids[None, None, :]
    return jnp.sum(jnp.where(named, combine[:, :, None], jnp.float32(0.0)), axis=1)


def outgoing_rows(slot_entries, out_grad, weight_table):
    experts, width = slot_entries.shape
    listed = slot_entries.reshape(-1)
    owned = out_grad.shape[0]
    selector = jnp.arange(owned, dtype=jnp.int32)[:, None] == listed[None, :]
    contract = (((0,), (0,)), ((), ()))
    selector_half = selector.astype(jnp.bfloat16)
    gathered = lax.dot_general(
        selector_half, out_grad, contract, preferred_element_type=jnp.float32
    )
    picked = lax.dot_general(
        selector.astype(jnp.float32),
        weight_table,
        contract,
        precision=lax.Precision.HIGHEST,
        preferred_element_type=jnp.float32,
    )
    slot_owner = jnp.arange(experts * width, dtype=jnp.int32) // width
    window_ids = jnp.arange(experts, dtype=jnp.int32)
    slot_weight = jnp.sum(
        jnp.where(slot_owner[:, None] == window_ids[None, :], picked, jnp.float32(0.0)), axis=1
    )
    outgoing = (
        (gathered * slot_weight[:, None])
        .astype(jnp.bfloat16)
        .reshape(experts, width, out_grad.shape[1])
    )
    return (outgoing, selector_half)


def on_device(
    out_grad, route_ids, combine, row_lists, saved_inputs, gate_weight, up_weight, down_weight
):
    experts = lax.axis_size("expert")
    batches = row_lists.shape[0]
    width = row_lists.shape[2]
    model_width = out_grad.shape[1]
    weight_table = token_weights(route_ids, combine, experts)
    accumulated = jnp.zeros(out_grad.shape, jnp.float32)
    prepared = [
        outgoing_rows(row_lists[batch_index], out_grad, weight_table)
        for batch_index in range(batches)
    ]
    stacked = jnp.stack([entry[0] for entry in prepared], axis=1)
    arrived = lax.all_to_all(stacked, "expert", split_axis=0, concat_axis=0, tiled=True)
    results = []
    for batch_index in range(batches):
        slot_grad = expert_backward(
            saved_inputs[batch_index, 0],
            arrived[:, batch_index].reshape(-1, model_width),
            gate_weight[0],
            up_weight[0],
            down_weight[0],
        )
        results.append(slot_grad.reshape(experts, width, model_width))
    returned = lax.all_to_all(
        jnp.stack(results, axis=1), "expert", split_axis=0, concat_axis=0, tiled=True
    )
    for batch_index in range(batches):
        accumulated = accumulated + jnp.dot(
            prepared[batch_index][1],
            returned[:, batch_index].reshape(-1, model_width),
            preferred_element_type=jnp.float32,
        )
    return accumulated.astype(jnp.bfloat16)


def solution(mesh):
    return jax.shard_map(
        on_device,
        mesh=mesh,
        in_specs=(
            P(("dp", "expert"), None),
            P(("dp", "expert"), None),
            P(("dp", "expert"), None),
            P("dp", None, "expert"),
            P("dp", "expert", None, None),
            P("expert", None, None),
            P("expert", None, None),
            P("expert", None, None),
        ),
        out_specs=P(("dp", "expert"), None),
        check_vma=False,
    )
```

profile of v0, /device:TPU:0, one launch (start us, length us, event | category | flops | bytes accessed | tf_op | source)
XLA Modules:
  0.0 67.4 jit_solution(16244251394436581457)
XLA Ops:
  0.0 0.0 copy-start
  0.0 0.0 copy-start.6
  0.0 0.8 %fusion.88 = (s32[1,4,48]{2,1,0:T(4,128)S(1)}, s32[1,4,48]{2,1,0:T(4,128)S(1)}) fusion(s32[2,4,48]{2,1,0:T(4,128)} %param.11), kind=kLoop, calls=%fused_computation.86 | loop fusion | bytes 3072 | tf_op jit(solution)/shard_map/slice | solution.py:75
  0.9 0.1 eq.70
  0.9 0.1 eq.80
  1.0 0.7 %select_reduce_fusion = f32[128,4]{0,1:T(4,128)S(1)} fusion(f32[128,8]{0,1:T(8,128)} %param.10, s32[128,8]{0,1:T(8,128)} %param.9), kind=kLoop, calls=%fused_computation.73 | loop fusion | flops 11776 | bytes 10240 | tf_op jit(solution)/shard_map/reduce_sum | solution.py:32
  1.8 0.2 fusion.51
  1.9 0.2 fusion.52
  2.1 1.5 %fusion.2 = bf16[192,2048]{1,0:T(8,128)(2,1)S(1)} fusion(bf16[128,2048]{1,0:T(8,128)(2,1)} %param.8, f32[192]{0:T(256)S(1)} %fusion.51, s32[192]{0:T(256)S(1)} %eq.70), kind=kOutput, calls=%fused_computation.6 | convolution fusion | flops 101474304 | bytes 1312256 | tf_op jit(solution)/shard_map/dot_general | solution.py:42
  3.6 0.0 copy-done.6
  3.6 0.4 fusion.3
  4.0 1.3 %pad_maximum_fusion = bf16[4,2,48,2048]{3,2,1,0:T(8,128)(2,1)} fusion(bf16[4,1,48,2048]{3,2,1,0:T(8,128)(2,1)S(1)} %bitcast.81, bf16[4,1,48,2048]{3,2,1,0:T(8,128)(2,1)S(1)} %bitcast.80), kind=kLoop, calls=%fused_computation.10 | loop fusion | flops 786432 | bytes 3145728 | tf_op jit(solution)/shard_map/stack | solution.py:78
  5.3 4.3 %all-to-all-start = ((bf16[4,2,48,2048]{3,2,1,0:T(8,128)(2,1)}), bf16[4,2,48,2048]{3,2,1,0:T(8,128)(2,1)S(1)}, u32[]{:S(2)}, u32[]{:S(2)}) async-start(bf16[4,2,48,2048]{3,2,1,0:T(8,128)(2,1)} %pad_maximum_fusion), calls=%async_computation | async-start | bytes 3145728 | tf_op jit(solution)/shard_map/all_to_all | solution.py:79
  9.6 0.0 copy-start.3
  9.6 3.0 %fusion.11 = f32[192,384]{1,0:T(8,128)} fusion(bf16[1,2048,384]{2,1,0:T(8,128)(2,1)} %param.13, bf16[2,1,192,2048]{3,2,1,0:T(8,128)(2,1)} %param.12), kind=kOutput, calls=%fused_computation.18 | convolution fusion | flops 301989888 | bytes 2654208 | tf_op jit(solution)/shard_map/dot_general | solution.py:9
  12.6 0.0 copy-done.3
  12.6 2.4 %fusion.7 = f32[192,384]{1,0:T(8,128)} fusion(bf16[1,2048,384]{2,1,0:T(8,128)(2,1)S(1)} %copy-done.3, bf16[2,1,192,2048]{3,2,1,0:T(8,128)(2,1)} %param.12), kind=kOutput, calls=%fused_computation.14 | convolution fusion | flops 301989888 | bytes 2654208 | tf_op jit(solution)/shard_map/dot_general | solution.py:9
  15.0 14.6 %all-to-all-done = bf16[4,2,48,2048]{3,2,1,0:T(8,128)(2,1)S(1)} async-done(((bf16[4,2,48,2048]{3,2,1,0:T(8,128)(2,1)}), bf16[4,2,48,2048]{3,2,1,0:T(8,128)(2,1)S(1)}, u32[]{:S(2)}, u32[]{:S(2)}) %all-to-all-start) | async-done | bytes 1572896 | tf_op jit(solution)/shard_map/all_to_all | solution.py:79
  29.6 0.0 copy-start.1
  29.6 1.0 %fusion.87 = (bf16[4,1,48,2048]{3,2,1,0:T(8,128)(2,1)S(1)}, bf16[4,1,48,2048]{3,2,1,0:T(8,128)(2,1)}) fusion(bf16[4,2,48,2048]{3,2,1,0:T(8,128)(2,1)S(1)} %all-to-all-done), kind=kLoop, calls=%fused_computation.85 | loop fusion | bytes 3145728 | tf_op jit(solution)/shard_map/slice | solution.py:84
  30.6 0.7 %copy-done.1 = bf16[1,384,2048]{2,1,0:T(8,128)(2,1)S(1)} copy-done((bf16[1,384,2048]{2,1,0:T(8,128)(2,1)S(1)}, bf16[1,384,2048]{2,1,0:T(8,128)(2,1)}, u32[]{:S(2)}) %copy-start.1) | copy-done | bytes 1572888
  31.3 0.7 fusion.21
  32.0 0.0 copy-done
  32.0 3.0 %fusion.9 = f32[192,2048]{1,0:T(8,128)S(1)} fusion(bf16[1,2048,384]{2,1,0:T(8,128)(2,1)} %param.13, f32[192,384]{1,0:T(8,128)S(1)} %fusion.21, bf16[1,2048,384]{2,1,0:T(8,128)(2,1)S(1)} %copy-done, bf16[2,1,192,2048]{3,2,1,0:T(8,128)(2,1)} %param.12, f32[192,384]{1,0:T(8,128)} %fusion.11), kind=kOutput, calls=%fused_computation.16 | convolution fusion | flops 604717056 | bytes 6094848 | tf_op jit(solution)/shard_map/dot_general | solution.py:20
  35.0 0.0 copy-start.2
  35.0 0.0 copy-start.5
  35.0 2.7 %fusion = bf16[192,2048]{1,0:T(8,128)(2,1)} fusion(f32[192,2048]{1,0:T(8,128)S(1)} %fusion.9, bf16[1,2048,384]{2,1,0:T(8,128)(2,1)S(1)} %copy-done, f32[192,384]{1,0:T(8,128)S(1)} %fusion.21, f32[192,384]{1,0:T(8,128)} %fusion.11), kind=kOutput, calls=%fused_computation.4 | convolution fusion | flops 303218688 | bytes 4521984 | tf_op jit(solution)/shard_map/dot_general | solution.py:23
  37.7 0.0 copy-done.2
  37.7 0.0 copy-done.5
  37.7 0.7 fusion.19
  38.4 3.0 %fusion.5 = f32[192,2048]{1,0:T(8,128)S(1)} fusion(bf16[1,2048,384]{2,1,0:T(8,128)(2,1)} %param.13, f32[192,384]{1,0:T(8,128)S(1)} %fusion.19, bf16[1,2048,384]{2,1,0:T(8,128)(2,1)S(1)} %copy-done, bf16[2,1,192,2048]{3,2,1,0:T(8,128)(2,1)} %param.12, f32[192,384]{1,0:T(8,128)} %fusion.7), kind=kOutput, calls=%fused_computation.12 | convolution fusion | flops 604717056 | bytes 6094848 | tf_op jit(solution)/shard_map/dot_general | solution.py:20
  41.3 0.0 copy-start.4
  41.3 1.7 %fusion.1 = bf16[192,2048]{1,0:T(8,128)(2,1)S(1)} fusion(f32[192,2048]{1,0:T(8,128)S(1)} %fusion.5, bf16[1,2048,384]{2,1,0:T(8,128)(2,1)S(1)} %copy-done, f32[192,384]{1,0:T(8,128)S(1)} %fusion.19, f32[192,384]{1,0:T(8,128)} %fusion.7), kind=kOutput, calls=%fused_computation.5 | convolution fusion | flops 303218688 | bytes 4521984 | tf_op jit(solution)/shard_map/dot_general | solution.py:23
  43.1 0.0 copy-done.4
  43.1 0.1 pad_maximum_fusion.1
  43.3 22.5 %all_to_all.10 = bf16[4,2,48,2048]{3,2,1,0:T(8,128)(2,1)S(1)} all-to-all(bf16[4,2,48,2048]{3,2,1,0:T(8,128)(2,1)S(1)} %pad_maximum_fusion.1), channel_id=1, replica_groups=mesh['expert'=4,'dp'=8] {'expert'}, dimensions={0} | all-to-all | bytes 3145728 | tf_op jit(solution)/shard_map/all_to_all | solution.py:90
  65.8 0.2 fusion.86
  65.9 0.3 fusion.75
  66.2 1.1 %fusion.4 = bf16[128,2048]{1,0:T(8,128)(2,1)} fusion(f32[128,2048]{1,0:T(8,128)S(1)} %fusion.75, bf16[192,2048]{1,0:T(8,128)(2,1)S(1)} %bitcast.82, s32[192]{0:T(256)S(1)} %eq.80), kind=kOutput, calls=%fused_computation.9 | convolution fusion | flops 101212160 | bytes 2360064 | tf_op jit(solution)/shard_map/dot_general | solution.py:94
  (1 shorter events, 0.0 us)
Async XLA Ops:
  0.0 32.0 %copy-start = (bf16[1,2048,384]{2,1,0:T(8,128)(2,1)S(1)}, bf16[1,2048,384]{2,1,0:T(8,128)(2,1)}, u32[]{:S(2)}) copy-start(bf16[1,2048,384]{2,1,0:T(8,128)(2,1)} %param.14) | copy-start | bytes 4718596
  0.0 3.6 %copy-start.6 = (bf16[128,2048]{1,0:T(8,128)(2,1)S(1)}, bf16[128,2048]{1,0:T(8,128)(2,1)}, u32[]{:S(2)}) copy-start(bf16[128,2048]{1,0:T(8,128)(2,1)} %param.8) | copy-start | bytes 1572868
  5.3 24.3 %all-to-all-start = ((bf16[4,2,48,2048]{3,2,1,0:T(8,128)(2,1)}), bf16[4,2,48,2048]{3,2,1,0:T(8,128)(2,1)S(1)}, u32[]{:S(2)}, u32[]{:S(2)}) async-start(bf16[4,2,48,2048]{3,2,1,0:T(8,128)(2,1)} %pad_maximum_fusion), calls=%async_computation | async-start | bytes 3145728 | tf_op jit(solution)/shard_map/all_to_all | solution.py:79
  9.6 3.0 %copy-start.3 = (bf16[1,2048,384]{2,1,0:T(8,128)(2,1)S(1)}, bf16[1,2048,384]{2,1,0:T(8,128)(2,1)}, u32[]{:S(2)}) copy-start(bf16[1,2048,384]{2,1,0:T(8,128)(2,1)} %param.13) | copy-start | bytes 4718596
  29.6 1.7 %copy-start.1 = (bf16[1,384,2048]{2,1,0:T(8,128)(2,1)S(1)}, bf16[1,384,2048]{2,1,0:T(8,128)(2,1)}, u32[]{:S(2)}) copy-start(bf16[1,384,2048]{2,1,0:T(8,128)(2,1)} %param.15) | copy-start | bytes 4718596
  35.0 2.7 %copy-start.2 = (bf16[1,384,2048]{2,1,0:T(8,128)(2,1)S(1)}, bf16[1,384,2048]{2,1,0:T(8,128)(2,1)}, u32[]{:S(2)}) copy-start(bf16[1,384,2048]{2,1,0:T(8,128)(2,1)} %param.15) | copy-start | bytes 4718596
  35.0 2.7 %copy-start.5 = (bf16[4,1,48,2048]{3,2,1,0:T(8,128)(2,1)S(1)}, bf16[4,1,48,2048]{3,2,1,0:T(8,128)(2,1)}, u32[]{:S(2)}) copy-start(bf16[4,1,48,2048]{3,2,1,0:T(8,128)(2,1)} %get-tuple-element.8) | copy-start | bytes 2359300
  41.3 1.8 %copy-start.4 = (bf16[192,2048]{1,0:T(8,128)(2,1)S(1)}, bf16[192,2048]{1,0:T(8,128)(2,1)}, u32[]{:S(2)}) copy-start(bf16[192,2048]{1,0:T(8,128)(2,1)} %fusion) | copy-start | bytes 2359300
where the time goes:
time: 67.8 us; the launch traced here: 67.4 us
  blocking collectives  22.5 us (33%)
  matrix products  20.8 us (31%)
  waiting for transfers between devices  14.6 us (22%)
  starting transfers between devices  4.26 us (6%)
  local copies, waits for them, and re-layouts  2.9 us (4%)
  other arithmetic  2.19 us (3%)
    all_to_all x1, blocking collectives, on_device(): lax.all_to_all(jnp.stack(results, axis=1), 'expert', split_axis=0, concat...  22.5 us
    all_to_all x1, waiting for transfers between devices, on_device(): lax.all_to_all(stacked, 'expert', split_axis=0, concat_axis=0, tiled=True)  14.6 us
    dot_general x2, matrix products, expert_backward(): lax.dot_general(grad_gate, gate_weight, contract, preferred_element_type=...  5.92 us
    dot_general x2, matrix products, expert_backward(): jnp.dot(saved_rows, gate_weight, preferred_element_type=jnp.float32)  5.46 us
    dot_general x2, matrix products, expert_backward(): lax.dot_general(grad_up, up_weight, contract, preferred_element_type=jnp....  4.47 us
    all_to_all x1, starting transfers between devices, on_device(): lax.all_to_all(stacked, 'expert', split_axis=0, concat_axis=0, tiled=True)  4.26 us
    dot_general x2, matrix products, outgoing_rows(): lax.dot_general(selector_half, out_grad, contract, preferred_element_type...  1.86 us
    dot_general x2, matrix products, on_device(): jnp.dot(prepared[batch_index][1], returned[:, batch_index].reshape(-1, mo...  1.41 us
  transfers between devices with their start and end apart: 1, of which 1 were waited for; matrix products, arithmetic and copies ran while one was open for 8% of the time, Pallas kernels for 0%

commit v1 on v0

v1 whole, which is shorter than its diff:
```python
import functools

import jax
import jax.numpy as jnp
from jax import lax
from jax.experimental import pallas as pl
from jax.experimental.pallas import tpu as pltpu
from jax.sharding import PartitionSpec as P

MESH = pl.DeviceIdType.MESH
BF16 = jnp.bfloat16
F32 = jnp.float32
CORES = 2


def kernel(
    n,
    og_ref, route_ref, combine_ref, lists_ref, saved_ref, gate_ref, up_ref, down_ref,
    out_ref,
    og, saved, gate, up, down, meta_out, meta_in, tokens_in, gate_factor, up_factor,
    part, part_in, back_out, back_in, own_sum,
    load_sem, meta_send, meta_recv, og_send, og_recv, part_send, part_recv, back_send, back_recv,
):
    chips = n // CORES
    batches, experts, width = lists_ref.shape
    slots = saved.shape[1]
    rows = og.shape[3]
    hidden = down.shape[0]
    lanes = meta_in.shape[3]
    me = lax.axis_index("expert")
    chip, core = me // CORES, me % CORES
    other = 1 - core

    def device(d, k):
        return {"expert": lax.rem(chip + d, chips) * CORES + (core if k == 0 else other)}

    partner = device(0, 1)

    def remote(src, dst, send, recv, target):
        return pltpu.make_async_remote_copy(
            src_ref=src, dst_ref=dst, send_sem=send, recv_sem=recv, device_id=target, device_id_type=MESH
        )

    barrier = pltpu.get_barrier_semaphore()
    places = [(d, k) for d in range(chips) for k in range(CORES)]
    others = places[1:]
    for d, k in others:
        pl.semaphore_signal(barrier, inc=1, device_id=device(d, k), device_id_type=MESH)

    loads = [
        pltpu.make_async_copy(saved_ref.at[:, 0], saved, load_sem.at[0]),
        pltpu.make_async_copy(gate_ref.at[0], gate, load_sem.at[1]),
        pltpu.make_async_copy(up_ref.at[0], up, load_sem.at[2]),
        pltpu.make_async_copy(down_ref.at[0], down, load_sem.at[3]),
    ]
    own = [
        pltpu.make_async_copy(og_ref.at[pl.ds(m * rows, rows)], og.at[0, 0, m], load_sem.at[4 + m])
        for m in range(batches)
    ]
    for copy in loads + own:
        copy.start()

    owned = og_ref.shape[0]
    route = route_ref[...]
    combine = combine_ref[...]
    lane = lax.broadcasted_iota(jnp.int32, (1, lanes), 1)
    mine = jnp.logical_and(lane >= me * width, lane < (me + 1) * width)
    pad = [jnp.full((1, lanes - slots), -1, jnp.int32)] if lanes > slots else []
    for d, k in places:
        target = device(d, k)["expert"]
        weight_row = jnp.sum(jnp.where(route == target, combine, 0.0), axis=0, keepdims=True)
        where = meta_in if (d, k) == (0, 0) else meta_out
        where[d, k, 0:1, 0:owned] = weight_row
        for m in range(batches):
            entries = lists_ref[m, pl.ds(target, 1), :]
            tiled = jnp.concatenate([entries] * experts + pad, axis=1)
            where[d, k, 1 + m : 2 + m, :] = jnp.where(mine, tiled, -1).astype(F32)

    pl.semaphore_wait(barrier, n - 1)

    sends = []

    def launch(copy):
        copy.start()
        sends.append(copy)
        return copy

    metas = {
        (d, k): launch(
            remote(meta_out.at[d, k], meta_in.at[d, k], meta_send.at[d, k], meta_recv.at[d, k], device(d, k))
        )
        for d, k in others
    }
    arrivals = {}
    for m in range(batches):
        part_rows = og_ref.at[pl.ds(m * rows, rows)]
        for d in range(1, chips):
            arrivals[d, 0, m] = launch(
                remote(part_rows, og.at[d, 0, m], og_send.at[d, 0, m], og_recv.at[d, 0, m], device(d, 0))
            )
        arrivals[0, 1, m] = launch(
            remote(part_rows, og.at[0, 1, m], og_send.at[0, 1, m], og_recv.at[0, 1, m], partner)
        )

    for place in others:
        metas[place].wait_recv()
    loads[0].wait()
    token = lax.broadcasted_iota(jnp.int32, (rows, slots), 0)
    for m in range(batches):
        wanted = (token + m * rows).astype(F32)
        for i, (d, k) in enumerate(places):
            listed = meta_in[d, k, 1 + m : 2 + m, 0:slots]
            select = jnp.where(listed == wanted, 1.0, 0.0).astype(BF16)
            tokens_in[m, i * rows : (i + 1) * rows, :] = jnp.dot(
                select, saved[m], preferred_element_type=F32
            ).astype(BF16)
    loads[1].wait()
    loads[2].wait()
    eye = lax.broadcasted_iota(jnp.int32, (rows, rows), 0) == lax.broadcasted_iota(
        jnp.int32, (rows, rows), 1
    )
    for m in range(batches):
        gate_value = jnp.dot(tokens_in[m], gate[...], preferred_element_type=F32)
        up_value = jnp.dot(tokens_in[m], up[...], preferred_element_type=F32)
        sigmoid = jax.nn.sigmoid(gate_value)
        columns = []
        for d, k in places:
            weight_row = meta_in[d, k, 0:1, m * rows : (m + 1) * rows]
            columns.append(
                jnp.sum(jnp.where(eye, weight_row, 0.0), axis=1, keepdims=True)
            )
        weight = jnp.concatenate(columns, axis=0)
        gate_factor[m] = weight * (up_value * sigmoid * (1.0 + gate_value * (1.0 - sigmoid)))
        up_factor[m] = weight * (gate_value * sigmoid)

    contract = (((1,), (1,)), ((), ()))

    def slot_grad(m, d, k, count=1):
        first = (d * CORES + k) * rows
        span = slice(first, first + count * rows)
        grads = og[d, k, m] if count == 1 else jnp.concatenate([og[d, k + j, m] for j in range(count)], axis=0)
        grad_hidden = lax.dot_general(grads, down[...], contract, preferred_element_type=F32)
        grad_gate = (grad_hidden * gate_factor[m, span, :]).astype(BF16)
        grad_up = (grad_hidden * up_factor[m, span, :]).astype(BF16)
        return lax.dot_general(grad_gate, gate[...], contract, preferred_element_type=F32) + lax.dot_general(
            grad_up, up[...], contract, preferred_element_type=F32
        )

    loads[3].wait()
    partials = {}
    for m in range(batches):
        own[m].wait()
        arrivals[0, 1, m].wait_recv()
        both = slot_grad(m, 0, 0, 2)
        own_sum[m] = both[0:rows]
        part[0, m] = both[rows : 2 * rows].astype(BF16)
        partials[0, m] = launch(
            remote(part.at[0, m], part_in.at[0, m], part_send.at[0, m], part_recv.at[0, m], partner)
        )

    backs = {}
    for m in range(batches):
        for d in range(1, chips):
            arrivals[d, 0, m].wait_recv()
            arrivals[d, 1, m] = launch(
                remote(og.at[d, 0, m], og.at[d, 1, m], og_send.at[d, 1, m], og_recv.at[d, 1, m], partner)
            )
        for d in range(1, chips):
            arrivals[d, 1, m].wait_recv()
            both = slot_grad(m, d, 0, 2)
            part[d, m] = both[rows : 2 * rows].astype(BF16)
            partials[d, m] = launch(
                remote(part.at[d, m], part_in.at[d, m], part_send.at[d, m], part_recv.at[d, m], partner)
            )
            mine_sum = both[0:rows].astype(BF16).astype(F32)
            partials[d, m].wait_recv()
            back_out[d, m] = (mine_sum + part_in[d, m].astype(F32)).astype(BF16)
            backs[d, m] = launch(
                remote(
                    back_out.at[d, m], back_in.at[d, m], back_send.at[d, m], back_recv.at[d, m],
                    device(chips - d, 0),
                )
            )

    for m in range(batches):
        partials[0, m].wait_recv()
        own_sum[m] = own_sum[m] + part_in[0, m].astype(F32)
    for m in range(batches):
        total = own_sum[m]
        for d in range(1, chips):
            backs[d, m].wait_recv()
            total = total + back_in[d, m].astype(F32)
        out_ref[m * rows : (m + 1) * rows, :] = total.astype(out_ref.dtype)
    for copy in sends:
        copy.wait_send()


def on_device(
    out_grad, route_ids, combine, row_lists, saved_inputs, gate_weight, up_weight, down_weight
):
    n = lax.axis_size("expert")
    chips = n // CORES
    batches = row_lists.shape[0]
    owned, width = out_grad.shape
    rows = owned // batches
    slots = saved_inputs.shape[2]
    hidden = gate_weight.shape[2]
    lanes = max(-(-slots // 128), -(-owned // 128)) * 128
    meta_rows = -(-(1 + batches) // 8) * 8
    hbm = pl.BlockSpec(memory_space=pl.ANY)
    vmem = pl.BlockSpec(memory_space=pltpu.VMEM)
    dma = pltpu.SemaphoreType.DMA
    return pl.pallas_call(
        functools.partial(kernel, n),
        out_shape=jax.ShapeDtypeStruct(out_grad.shape, out_grad.dtype),
        in_specs=[hbm, vmem, vmem, vmem, hbm, hbm, hbm, hbm],
        out_specs=vmem,
        scratch_shapes=[
            pltpu.VMEM((chips, CORES, batches, rows, width), BF16),
            pltpu.VMEM((batches, slots, width), BF16),
            pltpu.VMEM((width, hidden), BF16),
            pltpu.VMEM((width, hidden), BF16),
            pltpu.VMEM((hidden, width), BF16),
            pltpu.VMEM((chips, CORES, meta_rows, lanes), F32),
            pltpu.VMEM((chips, CORES, meta_rows, lanes), F32),
            pltpu.VMEM((batches, n * rows, width), BF16),
            pltpu.VMEM((batches, n * rows, hidden), F32),
            pltpu.VMEM((batches, n * rows, hidden), F32),
            pltpu.VMEM((chips, batches, rows, width), BF16),
            pltpu.VMEM((chips, batches, rows, width), BF16),
            pltpu.VMEM((chips, batches, rows, width), BF16),
            pltpu.VMEM((chips, batches, rows, width), BF16),
            pltpu.VMEM((batches, rows, width), F32),
            dma((4 + batches,)),
            dma((chips, CORES)),
            dma((chips, CORES)),
            dma((chips, CORES, batches)),
            dma((chips, CORES, batches)),
            dma((chips, batches)),
            dma((chips, batches)),
            dma((chips, batches)),
            dma((chips, batches)),
        ],
        compiler_params=pltpu.CompilerParams(
            collective_id=0, has_side_effects=True, vmem_limit_bytes=60 * 1024 * 1024
        ),
    )(out_grad, route_ids.T, combine.T, row_lists, saved_inputs, gate_weight, up_weight, down_weight)


def solution(mesh):
    return jax.shard_map(
        on_device,
        mesh=mesh,
        in_specs=(
            P(("dp", "expert"), None),
            P(("dp", "expert"), None),
            P(("dp", "expert"), None),
            P("dp", None, "expert"),
            P("dp", "expert", None, None),
            P("expert", None, None),
            P("expert", None, None),
            P("expert", None, None),
        ),
        out_specs=P(("dp", "expert"), None),
        check_vma=False,
    )
```

time: 67.8 us -> 35 us (0.52)
  Pallas kernels: 0 us -> 32.9 us
  blocking collectives: 22.5 us -> 0 us
  matrix products: 20.8 us -> 0 us
  waiting for transfers between devices: 14.6 us -> 0 us
  starting transfers between devices: 4.26 us -> 0 us
  other arithmetic: 2.19 us -> 0 us
  local copies, waits for them, and re-layouts: 2.9 us -> 1.88 us
    pallas_call x0 -> x1, Pallas kernels: none -> 32.9 us  [on_device(): pl.pallas_call(functools.partial(kernel, n), out_shape=jax.ShapeDtypeStru...]
    all_to_all x1 -> x0, blocking collectives: 22.5 us -> none  [on_device(): lax.all_to_all(jnp.stack(results, axis=1), 'expert', split_axis=0, concat...]
    dot_general x14 -> x0, matrix products: 20.8 us -> none  [the longest x2 5.92 us: expert_backward(): lax.dot_general(grad_gate, gate_weight, contract, preferred_element_type=...]
    all_to_all x1 -> x0, waiting for transfers between devices: 14.6 us -> none  [on_device(): lax.all_to_all(stacked, 'expert', split_axis=0, concat_axis=0, tiled=True)]
    all_to_all x1 -> x0, starting transfers between devices: 4.26 us -> none  [on_device(): lax.all_to_all(stacked, 'expert', split_axis=0, concat_axis=0, tiled=True)]
    slice x3 -> x0, local copies, waits for them, and re-layouts: 2.01 us -> none  [the longest x1 1 us: on_device(): arrived[:, batch_index].reshape(-1, model_width)]
    another operation x2 -> x0, other arithmetic: 1.46 us -> none  [the longest x1 1.31 us: on_device(): stacked = jnp.stack([entry[0] for entry in prepared], axis=1)]
    unnamed x14 -> x1, local copies, waits for them, and re-layouts: 0.72 us -> 1.88 us
  transfers between devices with their start and end apart: 1 -> 0, of which waited for: 1 -> 0; matrix products, arithmetic and copies ran while one was open for 8% -> 0% of each run, Pallas kernels for 0% -> 0%
where the time goes in v1:
time: 35 us; the launch traced here: 34.8 us
  Pallas kernels  32.9 us (94%)
  local copies, waits for them, and re-layouts  1.88 us (5%)
    pallas_call x1, Pallas kernels, on_device(): pl.pallas_call(functools.partial(kernel, n), out_shape=jax.ShapeDtypeStru...  32.9 us
    unnamed x1, local copies, waits for them, and re-layouts  1.88 us

profile of v1, /device:TPU:0, one launch (start us, length us, event | category | flops | bytes accessed | tf_op | source)
XLA Modules:
  0.0 34.8 jit_solution(8631078768134356398)
XLA Ops:
  0.0 32.9 %shard_map.82 = bf16[128,2048]{1,0:T(8,128)(2,1)} custom-call(bf16[128,2048]{1,0:T(8,128)(2,1)} %og_ref.1, s32[8,128]{1,0:T(8,128)} %bitcast.2, f32[8,128]{1,0:T(8,128)} %bitcast.3, s32[2,4,48]{2,1,0:T(4,128)} %lists_ref.1, bf16[2,1,192,2048]{3,2,1,0:T(8,128)(2,1)} %saved_ref.1, bf16[1,2048,384]{2,1,0:T(8,128)(2,1)} %gate_ref.1, ...), custom_call_target="tpu_custom_call" | custom-call | tf_op jit(solution)/shard_map/pallas_call | solution.py:213
  32.9 1.9 %copy.10 = bf16[128,2048]{1,0:T(8,128)(2,1)} copy(bf16[128,2048]{1,0:T(8,128)(2,1)} %shard_map.82) | data formatting | bytes 1048576

commit v2 on v1

--- a/solution.py
+++ b/solution.py
@@ -14,11 +14,12 @@
 
 
 def kernel(
-    n,
+    n, splits,
     og_ref, route_ref, combine_ref, lists_ref, saved_ref, gate_ref, up_ref, down_ref,
     out_ref,
     og, saved, gate, up, down, meta_out, meta_in, tokens_in, gate_factor, up_factor,
-    part, part_in, back_out, back_in, own_sum,
+    part, part_own, part_in, back_in, own_sum,
+    down_t, pair_t,
     load_sem, meta_send, meta_recv, og_send, og_recv, part_send, part_recv, back_send, back_recv,
 ):
     chips = n // CORES
@@ -91,106 +92,150 @@
         )
         for d, k in others
     }
+    distances = range(1, chips)
+    pieces = []
+    for m in range(batches):
+        cuts = splits[m]
+        pieces += [(m, pl.ds(i * (rows // cuts), rows // cuts), i * (rows // cuts)) for i in range(cuts)]
+    numbered = list(enumerate(pieces))
     arrivals = {}
-    for m in range(batches):
-        part_rows = og_ref.at[pl.ds(m * rows, rows)]
-        for d in range(1, chips):
-            arrivals[d, 0, m] = launch(
-                remote(part_rows, og.at[d, 0, m], og_send.at[d, 0, m], og_recv.at[d, 0, m], device(d, 0))
+    for p, (m, span, first) in numbered:
+        for d in distances:
+            arrivals[d, 0, p] = launch(
+                remote(
+                    og_ref.at[pl.ds(m * rows + first, span.size)], og.at[d, 0, m, span],
+                    og_send.at[d, 0, p], og_recv.at[d, 0, p], device(d, 0),
+                )
             )
-        arrivals[0, 1, m] = launch(
-            remote(part_rows, og.at[0, 1, m], og_send.at[0, 1, m], og_recv.at[0, 1, m], partner)
-        )
-
-    for place in others:
-        metas[place].wait_recv()
-    loads[0].wait()
+        if first == 0:
+            arrivals[0, 1, m] = launch(
+                remote(
+                    og_ref.at[pl.ds(m * rows, rows)], og.at[0, 1, m],
+                    og_send.at[0, 1, m], og_recv.at[0, 1, m], partner,
+                )
+            )
+
     token = lax.broadcasted_iota(jnp.int32, (rows, slots), 0)
-    for m in range(batches):
+    eye = lax.broadcasted_iota(jnp.int32, (rows, rows), 0) == lax.broadcasted_iota(
+        jnp.int32, (rows, rows), 1
+    )
+
+    def factors(m):
         wanted = (token + m * rows).astype(F32)
+        columns = []
         for i, (d, k) in enumerate(places):
             listed = meta_in[d, k, 1 + m : 2 + m, 0:slots]
             select = jnp.where(listed == wanted, 1.0, 0.0).astype(BF16)
             tokens_in[m, i * rows : (i + 1) * rows, :] = jnp.dot(
                 select, saved[m], preferred_element_type=F32
             ).astype(BF16)
-    loads[1].wait()
-    loads[2].wait()
-    eye = lax.broadcasted_iota(jnp.int32, (rows, rows), 0) == lax.broadcasted_iota(
-        jnp.int32, (rows, rows), 1
-    )
-    for m in range(batches):
+            weight_row = meta_in[d, k, 0:1, m * rows : (m + 1) * rows]
+            columns.append(jnp.sum(jnp.where(eye, weight_row, 0.0), axis=1, keepdims=True))
+        if m == 0:
+            loads[1].wait()
+            loads[2].wait()
         gate_value = jnp.dot(tokens_in[m], gate[...], preferred_element_type=F32)
         up_value = jnp.dot(tokens_in[m], up[...], preferred_element_type=F32)
         sigmoid = jax.nn.sigmoid(gate_value)
-        columns = []
-        for d, k in places:
-            weight_row = meta_in[d, k, 0:1, m * rows : (m + 1) * rows]
-            columns.append(
-                jnp.sum(jnp.where(eye, weight_row, 0.0), axis=1, keepdims=True)
-            )
         weight = jnp.concatenate(columns, axis=0)
         gate_factor[m] = weight * (up_value * sigmoid * (1.0 + gate_value * (1.0 - sigmoid)))
         up_factor[m] = weight * (gate_value * sigmoid)
 
-    contract = (((1,), (1,)), ((), ()))
-
-    def slot_grad(m, d, k, count=1):
-        first = (d * CORES + k) * rows
-        span = slice(first, first + count * rows)
-        grads = og[d, k, m] if count == 1 else jnp.concatenate([og[d, k + j, m] for j in range(count)], axis=0)
-        grad_hidden = lax.dot_general(grads, down[...], contract, preferred_element_type=F32)
-        grad_gate = (grad_hidden * gate_factor[m, span, :]).astype(BF16)
-        grad_up = (grad_hidden * up_factor[m, span, :]).astype(BF16)
-        return lax.dot_general(grad_gate, gate[...], contract, preferred_element_type=F32) + lax.dot_general(
-            grad_up, up[...], contract, preferred_element_type=F32
-        )
-
-    loads[3].wait()
-    partials = {}
-    for m in range(batches):
+
+    def slot_grad(m, d, first, count):
+        starts = [(d * CORES + k) * rows + first for k in range(CORES)]
+
+        def both_cores(ref):
+            return jnp.concatenate([ref[m, i : i + count, :] for i in starts], axis=0)
+
+        grads = jnp.concatenate([og[d, k, m, first : first + count, :] for k in range(CORES)], axis=0)
+        grad_hidden = jnp.dot(grads, down_t[...], preferred_element_type=F32)
+        grad_gate = (grad_hidden * both_cores(gate_factor)).astype(BF16)
+        grad_up = (grad_hidden * both_cores(up_factor)).astype(BF16)
+        pair = jnp.concatenate([grad_gate, grad_up], axis=1)
+        return jnp.dot(pair, pair_t[...], preferred_element_type=F32)
+
+    partials, backs = {}, {}
+
+    def exchange(p, m, d, span):
+        copy = remote(
+            part.at[d, m, span], part_in.at[d, m, span], part_send.at[d, p], part_recv.at[d, p], partner
+        )
+        partials[d, p] = launch(copy)
+
+    def near(m):
         own[m].wait()
         arrivals[0, 1, m].wait_recv()
-        both = slot_grad(m, 0, 0, 2)
+        both = slot_grad(m, 0, 0, rows)
+        part[0, m] = both[rows : 2 * rows].astype(BF16)
+        exchange(m, m, 0, pl.ds(0, rows))
         own_sum[m] = both[0:rows]
-        part[0, m] = both[rows : 2 * rows].astype(BF16)
-        partials[0, m] = launch(
-            remote(part.at[0, m], part_in.at[0, m], part_send.at[0, m], part_recv.at[0, m], partner)
-        )
-
-    backs = {}
-    for m in range(batches):
-        for d in range(1, chips):
-            arrivals[d, 0, m].wait_recv()
-            arrivals[d, 1, m] = launch(
-                remote(og.at[d, 0, m], og.at[d, 1, m], og_send.at[d, 1, m], og_recv.at[d, 1, m], partner)
+
+    def relay(p, d):
+        m, span, first = pieces[p]
+        arrivals[d, 0, p].wait_recv()
+        arrivals[d, 1, p] = launch(
+            remote(
+                og.at[d, 0, m, span], og.at[d, 1, m, span], og_send.at[d, 1, p], og_recv.at[d, 1, p], partner
             )
-        for d in range(1, chips):
-            arrivals[d, 1, m].wait_recv()
-            both = slot_grad(m, d, 0, 2)
-            part[d, m] = both[rows : 2 * rows].astype(BF16)
-            partials[d, m] = launch(
-                remote(part.at[d, m], part_in.at[d, m], part_send.at[d, m], part_recv.at[d, m], partner)
+        )
+
+    def far(p, d):
+        m, span, first = pieces[p]
+        count = span.size
+        arrivals[d, 1, p].wait_recv()
+        both = slot_grad(m, d, first, count)
+        part[d, m, first : first + count, :] = both[count : 2 * count].astype(BF16)
+        exchange(p, m, d, span)
+        part_own[d, m, first : first + count, :] = both[0:count].astype(BF16)
+
+    def give_back(p, d):
+        m, span, first = pieces[p]
+        here = slice(first, first + span.size)
+        partials[d, p].wait_recv()
+        part_own[d, m, here, :] = (part_own[d, m, here, :].astype(F32) + part_in[d, m, here, :].astype(F32)).astype(
+            BF16
+        )
+        backs[d, p] = launch(
+            remote(
+                part_own.at[d, m, span], back_in.at[d, m, span], back_send.at[d, p], back_recv.at[d, p],
+                device(chips - d, 0),
             )
-            mine_sum = both[0:rows].astype(BF16).astype(F32)
-            partials[d, m].wait_recv()
-            back_out[d, m] = (mine_sum + part_in[d, m].astype(F32)).astype(BF16)
-            backs[d, m] = launch(
-                remote(
-                    back_out.at[d, m], back_in.at[d, m], back_send.at[d, m], back_recv.at[d, m],
-                    device(chips - d, 0),
-                )
-            )
-
+        )
+
+    for place in others:
+        metas[place].wait_recv()
+    loads[0].wait()
+    factors(0)
+    loads[3].wait()
+    down_t[...] = down[...].T
+    pair_t[0:hidden, :] = gate[...].T
+    pair_t[hidden : 2 * hidden, :] = up[...].T
+    near(0)
+    for p, (m, span, first) in numbered:
+        for d in distances:
+            relay(p, d)
+        if p > 0:
+            for d in distances:
+                give_back(p - 1, d)
+        if first + span.size == rows and m + 1 < batches:
+            factors(m + 1)
+        for d in distances:
+            far(p, d)
+    for m in range(1, batches):
+        near(m)
+    for d in distances:
+        give_back(len(pieces) - 1, d)
     for m in range(batches):
         partials[0, m].wait_recv()
         own_sum[m] = own_sum[m] + part_in[0, m].astype(F32)
-    for m in range(batches):
-        total = own_sum[m]
-        for d in range(1, chips):
-            backs[d, m].wait_recv()
-            total = total + back_in[d, m].astype(F32)
-        out_ref[m * rows : (m + 1) * rows, :] = total.astype(out_ref.dtype)
+    for p, (m, span, first) in numbered:
+        here = slice(first, first + span.size)
+        total = own_sum[m, here, :]
+        for d in distances:
+            backs[d, p].wait_recv()
+            total = total + back_in[d, m, here, :].astype(F32)
+        out_ref[m * rows + first : m * rows + first + span.size, :] = total.astype(out_ref.dtype)
     for copy in sends:
         copy.wait_send()
 
@@ -207,11 +252,13 @@
     hidden = gate_weight.shape[2]
     lanes = max(-(-slots // 128), -(-owned // 128)) * 128
     meta_rows = -(-(1 + batches) // 8) * 8
+    splits = [2] * batches
+    count = sum(splits)
     hbm = pl.BlockSpec(memory_space=pl.ANY)
     vmem = pl.BlockSpec(memory_space=pltpu.VMEM)
     dma = pltpu.SemaphoreType.DMA
     return pl.pallas_call(
-        functools.partial(kernel, n),
+        functools.partial(kernel, n, splits),
         out_shape=jax.ShapeDtypeStruct(out_grad.shape, out_grad.dtype),
         in_specs=[hbm, vmem, vmem, vmem, hbm, hbm, hbm, hbm],
         out_specs=vmem,
@@ -231,15 +278,17 @@
             pltpu.VMEM((chips, batches, rows, width), BF16),
             pltpu.VMEM((chips, batches, rows, width), BF16),
             pltpu.VMEM((batches, rows, width), F32),
+            pltpu.VMEM((width, hidden), BF16),
+            pltpu.VMEM((2 * hidden, width), BF16),
             dma((4 + batches,)),
             dma((chips, CORES)),
             dma((chips, CORES)),
-            dma((chips, CORES, batches)),
-            dma((chips, CORES, batches)),
-            dma((chips, batches)),
-            dma((chips, batches)),
-            dma((chips, batches)),
-            dma((chips, batches)),
+            dma((chips, CORES, count)),
+            dma((chips, CORES, count)),
+            dma((chips, count)),
+            dma((chips, count)),
+            dma((chips, count)),
+            dma((chips, count)),
         ],
         compiler_params=pltpu.CompilerParams(
             collective_id=0, has_side_effects=True, vmem_limit_bytes=60 * 1024 * 1024

time: 35 us -> 32.8 us (0.937)
  Pallas kernels: 32.9 us -> 30.7 us
    pallas_call x1, Pallas kernels: 32.9 us -> 30.7 us  [on_device(): pl.pallas_call(functools.partial(kernel, n, splits), out_shape=jax.ShapeD...]
where the time goes in v2:
time: 32.8 us; the launch traced here: 32.5 us
  Pallas kernels  30.7 us (94%)
  local copies, waits for them, and re-layouts  1.88 us (6%)
    pallas_call x1, Pallas kernels, on_device(): pl.pallas_call(functools.partial(kernel, n, splits), out_shape=jax.ShapeD...  30.7 us
    unnamed x1, local copies, waits for them, and re-layouts  1.88 us

profile of v2, /device:TPU:0, one launch (start us, length us, event | category | flops | bytes accessed | tf_op | source)
XLA Modules:
  0.0 32.5 jit_solution(16574403072551867517)
XLA Ops:
  0.0 30.7 %shard_map.82 = bf16[128,2048]{1,0:T(8,128)(2,1)} custom-call(bf16[128,2048]{1,0:T(8,128)(2,1)} %og_ref.1, s32[8,128]{1,0:T(8,128)} %bitcast.2, f32[8,128]{1,0:T(8,128)} %bitcast.3, s32[2,4,48]{2,1,0:T(4,128)} %lists_ref.1, bf16[2,1,192,2048]{3,2,1,0:T(8,128)(2,1)} %saved_ref.1, bf16[1,2048,384]{2,1,0:T(8,128)(2,1)} %gate_ref.1, ...), custom_call_target="tpu_custom_call" | custom-call | tf_op jit(solution)/shard_map/pallas_call | solution.py:260
  30.7 1.9 %copy.10 = bf16[128,2048]{1,0:T(8,128)(2,1)} copy(bf16[128,2048]{1,0:T(8,128)(2,1)} %shard_map.82) | data formatting | bytes 1048576
